TPU v7x, 32 devices: a whole 2x2x4 slice. The times are simulated.
32 devices in a mesh: league: 4 (over x, core), env: 8 (over z, y).
Axes of the slice: x: 2, y: 2, z: 4, core: 2. Of those that a mesh axis runs over, the one named last changes fastest.
Arguments:
- obs_own: bfloat16 [4, 2, 128, 16, 2048], P('league', None, 'env'), may hold values from -6 to 6
- obs_opp: bfloat16 [4, 2, 128, 16, 2048], P('league', None, 'env'), may hold values from -6 to 6
- actions: int32 [4, 2, 2, 128, 16], P('league', None, None, 'env'), may hold values from 0 to 255
- opponent_picks: int32 [4, 2], P('league'), may hold values from 0 to 3
- policy_weight: bfloat16 [4, 2048, 2048], P('league', 'env'), may hold values from -0.125 to 0.125
- policy_gain: bfloat16 [4, 2048], P('league'), may hold values from 0.25 to 1.75
- action_table: bfloat16 [256, 2048], replicated, may hold values from -6 to 6
- value_gain: bfloat16 [2048], replicated, may hold values from 0.25 to 1.75
- value_up: bfloat16 [2048, 1024], replicated, may hold values from -0.125 to 0.125
- value_out: bfloat16 [1024], replicated, may hold values from -0.1875 to 0.1875
Outputs:
- learner_rows: bfloat16 [4, 2, 16, 2048, 128], P('league', None, None, 'env')
- values: float32 [4, 2, 128, 16], P('league', None, 'env')
All inputs are finite; a program needn't handle non-finite values.
Results may differ from a plain program's by a relative error of at most 0.0054.
Values may be sent and summed in bfloat16 or wider, within the bound.
A program may use at most 128 MiB of HBM per device.

v0:
```python
import jax
import jax.numpy as jnp
from jax import lax
from jax.sharding import PartitionSpec as P


def rms_norm(inputs, gain):
    scale = lax.rsqrt(jnp.mean(inputs * inputs, axis=-1, keepdims=True) + 1e-05)
    return inputs * scale * gain.astype(jnp.float32)


def local(
    obs_own,
    obs_opp,
    actions,
    opponent_picks,
    policy_weight,
    policy_gain,
    action_table,
    value_gain,
    value_up,
    value_out,
):
    round_count = obs_own.shape[1]
    env_count = obs_own.shape[2]
    step_count = obs_own.shape[3]
    model_width = obs_own.shape[4]
    row_count = env_count * step_count
    weight_shard = policy_weight[0]
    own_gain = policy_gain[0]
    group_count = lax.axis_size("league")
    my_group = lax.axis_index("league")
    own_inputs = obs_own[0].reshape(round_count * row_count, model_width).astype(jnp.float32)
    own_normed = rms_norm(own_inputs, own_gain).astype(jnp.bfloat16)
    own_whole = lax.all_gather(weight_shard, "env", axis=0, tiled=True)
    own_state = own_inputs + jnp.dot(own_normed, own_whole, preferred_element_type=jnp.float32)
    every_pick = lax.all_gather(opponent_picks, "league", axis=0, tiled=True)
    action_range = jnp.arange(action_table.shape[0], dtype=jnp.int32)
    traj_list = []
    value_list = []
    for round_index in range(round_count):
        opp_raw = obs_opp[0, round_index].reshape(row_count, model_width)
        opp_inputs = opp_raw.astype(jnp.float32)
        all_rows = lax.all_gather(opp_raw, "league", axis=0, tiled=True)
        all_normed = rms_norm(all_rows.astype(jnp.float32), own_gain).astype(jnp.bfloat16)
        products = jnp.dot(all_normed, own_whole, preferred_element_type=jnp.float32)
        served = (every_pick[:, round_index] == my_group).astype(jnp.float32)
        products = (
            products.reshape(group_count, row_count, model_width) * served[:, None, None]
        ).astype(jnp.bfloat16)
        answers = lax.all_to_all(products, "league", split_axis=0, concat_axis=0, tiled=True)
        opp_state = opp_inputs + jnp.sum(answers.astype(jnp.float32), axis=0)
        own_ids = actions[0, 0, round_index].reshape(row_count)
        opp_ids = actions[0, 1, round_index].reshape(row_count)
        onehot = (own_ids[:, None] == action_range[None, :]).astype(jnp.bfloat16) + (
            opp_ids[:, None] == action_range[None, :]
        ).astype(jnp.bfloat16)
        action_sum = jnp.dot(onehot, action_table, preferred_element_type=jnp.float32)
        round_state = lax.dynamic_slice_in_dim(own_state, round_index * row_count, row_count, 0)
        joint_sum = round_state + opp_state + action_sum
        joint_row = rms_norm(joint_sum, value_gain).astype(jnp.bfloat16)
        value_hidden = jax.nn.silu(
            jnp.dot(joint_row, value_up, preferred_element_type=jnp.float32)
        ).astype(jnp.bfloat16)
        value_est = jnp.dot(value_hidden, value_out, preferred_element_type=jnp.float32)
        value_list.append(value_est.reshape(env_count, step_count))
        time_block = joint_row.reshape(env_count, step_count, model_width).transpose(1, 2, 0)
        traj_list.append(lax.all_to_all(time_block, "env", split_axis=1, concat_axis=2, tiled=True))
    learner_rows = jnp.stack(traj_list)
    values = jnp.stack(value_list)
    return (learner_rows[None], values[None])


def solution(mesh):
    in_specs = (
        P("league", None, "env", None, None),
        P("league", None, "env", None, None),
        P("league", None, None, "env", None),
        P("league", None),
        P("league", "env", None),
        P("league", None),
        P(),
        P(),
        P(),
        P(),
    )
    out_specs = (P("league", None, None, "env", None), P("league", None, "env", None))
    return jax.shard_map(local, mesh=mesh, in_specs=in_specs, out_specs=out_specs, check_vma=False)
```

profile of v0, /device:TPU:0, one launch (start us, length us, event | category | flops | bytes accessed | tf_op | source)
XLA Modules:
  0.0 430.5 jit_solution(11888221236370943280)
XLA Ops:
  12.0 6.0 %all-gather.1 = s32[4,1,2]{2,1,0:T(1,128)S(1)} all-gather(s32[1,1,2]{2,1,0:T(1,128)S(1)} %bitcast.90), channel_id=1, replica_groups=mesh['league'=4,'env'=8] {'league'}, dimensions={0}, use_global_device_ids=true | all-gather | bytes 40 | tf_op jit(solution)/shard_map/all_gather | solution.py:37
  18.0 29.8 %all-gather.6.cloned.1.call-done = bf16[1024,2048]{1,0:T(8,128)(2,1)} async-done(((bf16[256,2048]{1,0:T(8,128)(2,1)}), bf16[1024,2048]{1,0:T(8,128)(2,1)}) %all-gather.6.cloned.1.call-update) | async-done | bytes 4194320 | tf_op jit(solution)/shard_map/all_gather | solution.py:44
  50.9 124.0 %all-gather.10.cloned.1.call-done = bf16[1,2048,2048]{2,1,0:T(8,128)(2,1)} async-done(((bf16[1,256,2048]{2,1,0:T(8,128)(2,1)}), bf16[1,2048,2048]{2,1,0:T(8,128)(2,1)}) %all-gather.10.cloned.1.call-update) | async-done | bytes 8388624 | tf_op jit(solution)/shard_map/all_gather | solution.py:35
  174.9 12.6 %fusion.8 = f32[1024,2048]{1,0:T(8,128)S(1)} fusion(bf16[1,2048,2048]{2,1,0:T(8,128)(2,1)} %all-gather.10.cloned.1.call-done, bf16[1024,2048]{1,0:T(8,128)(2,1)} %all-gather.6.cloned.1.call-done, f32[2048]{0:T(1024)S(1)} %bitcast.84, f32[1024]{0:T(1024)S(1)} %add_rsqrt_fusion.2), kind=kOutput, calls=%fused_computation.12 | convolution fusion | flops 8598323200 | bytes 20983808 | tf_op jit(solution)/shard_map/dot_general | solution.py:46
  190.7 4.9 %all-to-all-start = ((bf16[4,256,2048]{2,1,0:T(8,128)(2,1)}), bf16[4,256,2048]{2,1,0:T(8,128)(2,1)}, u32[]{:S(2)}, u32[]{:S(2)}) async-start(bf16[4,256,2048]{2,1,0:T(8,128)(2,1)} %multiply_convert_fusion.1), calls=%async_computation | async-start | bytes 8388608 | tf_op jit(solution)/shard_map/all_to_all | solution.py:51
  195.6 22.4 %all-gather.8.cloned.1.call-done = bf16[1024,2048]{1,0:T(8,128)(2,1)} async-done(((bf16[256,2048]{1,0:T(8,128)(2,1)}), bf16[1024,2048]{1,0:T(8,128)(2,1)}) %all-gather.8.cloned.1.call-update) | async-done | bytes 4194320 | tf_op jit(solution)/shard_map/all_gather | solution.py:44
  221.4 11.3 %fusion.6 = f32[1024,2048]{1,0:T(8,128)S(1)} fusion(bf16[1,2048,2048]{2,1,0:T(8,128)(2,1)} %all-gather.10.cloned.1.call-done, bf16[1024,2048]{1,0:T(8,128)(2,1)S(1)} %copy-done.7, f32[1024]{0:T(1024)S(1)} %add_rsqrt_fusion.1, f32[2048]{0:T(1024)S(1)} %bitcast.85), kind=kOutput, calls=%fused_computation.10 | convolution fusion | flops 8598323200 | bytes 20983808 | tf_op jit(solution)/shard_map/dot_general | solution.py:46
  235.9 16.6 %all-to-all-done = bf16[4,256,2048]{2,1,0:T(8,128)(2,1)} async-done(((bf16[4,256,2048]{2,1,0:T(8,128)(2,1)}), bf16[4,256,2048]{2,1,0:T(8,128)(2,1)}, u32[]{:S(2)}, u32[]{:S(2)}) %all-to-all-start) | async-done | bytes 4194336 | tf_op jit(solution)/shard_map/all_to_all | solution.py:51
  252.6 5.0 %all-to-all-start.2 = ((bf16[4,256,2048]{2,1,0:T(8,128)(2,1)}), bf16[4,256,2048]{2,1,0:T(8,128)(2,1)}, u32[]{:S(2)}, u32[]{:S(2)}) async-start(bf16[4,256,2048]{2,1,0:T(8,128)(2,1)} %multiply_convert_fusion), calls=%async_computation.2 | async-start | bytes 8388608 | tf_op jit(solution)/shard_map/all_to_all | solution.py:51
  259.1 7.0 %bitcast_add_fusion = f32[512,2048]{1,0:T(8,128)S(1)} fusion(bf16[1,2,16,16,2048]{4,3,2,1,0:T(8,128)(2,1)S(1)} %copy-done.4, bf16[512,2048]{1,0:T(8,128)(2,1)S(1)} %fusion.16, bf16[1,2048,2048]{2,1,0:T(8,128)(2,1)} %all-gather.10.cloned.1.call-done), kind=kOutput, calls=%fused_computation.20 | convolution fusion | flops 4297064448 | bytes 16777216 | tf_op jit(solution)/shard_map/dot_general | solution.py:36
  266.1 4.8 %convert_reduce_fusion.1 = f32[256,2048]{1,0:T(8,128)S(1)} fusion(bf16[4,256,2048]{2,1,0:T(8,128)(2,1)} %all-to-all-done), kind=kLoop, calls=%fused_computation.18 | loop fusion | flops 3670016 | bytes 6291456 | tf_op jit(solution)/shard_map/reduce_sum | solution.py:52
  273.1 32.6 %all-to-all-done.2 = bf16[4,256,2048]{2,1,0:T(8,128)(2,1)} async-done(((bf16[4,256,2048]{2,1,0:T(8,128)(2,1)}), bf16[4,256,2048]{2,1,0:T(8,128)(2,1)}, u32[]{:S(2)}, u32[]{:S(2)}) %all-to-all-start.2) | async-done | bytes 4194336 | tf_op jit(solution)/shard_map/all_to_all | solution.py:51
  311.2 8.8 %copy.27 = bf16[16,16,2048]{0,1,2:T(8,128)(2,1)} copy(bf16[16,16,2048]{2,1,0:T(8,128)(2,1)S(1)} %bitcast.81) | data formatting | bytes 2097152 | tf_op jit(solution)/shard_map/reshape | solution.py:67
  320.0 7.5 %bitcast_bitcast_fusion = bf16[2048,16,16]{2,1,0:T(8,128)(2,1)} fusion(bf16[16,16,2048]{0,1,2:T(8,128)(2,1)} %copy.27), kind=kLoop, calls=%fused_computation.71 | loop fusion | bytes 2097152
  327.5 11.2 %reshape.109 = bf16[8,2,32768]{2,1,0:T(2,128)(2,1)} reshape(bf16[2048,16,16]{2,1,0:T(8,128)(2,1)} %bitcast_bitcast_fusion) | data formatting | bytes 2097152
  338.7 5.5 %all-to-all-start.3 = ((bf16[8,2,32768]{2,1,0:T(2,128)(2,1)}), bf16[8,2,32768]{2,1,0:T(2,128)(2,1)S(1)}, u32[]{:S(2)}, u32[]{:S(2)}) async-start(bf16[8,2,32768]{2,1,0:T(2,128)(2,1)} %reshape.109), calls=%async_computation.3 | async-start | bytes 2097152 | tf_op jit(solution)/shard_map/all_to_all | solution.py:68
  344.2 8.8 %copy.24 = bf16[16,16,2048]{0,1,2:T(8,128)(2,1)} copy(bf16[16,16,2048]{2,1,0:T(8,128)(2,1)S(1)} %bitcast.80) | data formatting | bytes 2097152 | tf_op jit(solution)/shard_map/reshape | solution.py:67
  353.1 7.5 %bitcast_bitcast_fusion.1 = bf16[2048,16,16]{2,1,0:T(8,128)(2,1)} fusion(bf16[16,16,2048]{0,1,2:T(8,128)(2,1)} %copy.24), kind=kLoop, calls=%fused_computation.72 | loop fusion | bytes 2097152
  360.5 11.2 %reshape.111 = bf16[8,2,32768]{2,1,0:T(2,128)(2,1)} reshape(bf16[2048,16,16]{2,1,0:T(8,128)(2,1)} %bitcast_bitcast_fusion.1) | data formatting | bytes 2097152
  371.8 6.0 %all-to-all-start.1 = ((bf16[8,2,32768]{2,1,0:T(2,128)(2,1)}), bf16[8,2,32768]{2,1,0:T(2,128)(2,1)S(1)}, u32[]{:S(2)}, u32[]{:S(2)}) async-start(bf16[8,2,32768]{2,1,0:T(2,128)(2,1)} %reshape.111), calls=%async_computation.1 | async-start | bytes 2097152 | tf_op jit(solution)/shard_map/all_to_all | solution.py:68
  386.5 7.6 %reshape.110 = bf16[2048,16,16]{2,1,0:T(8,128)(2,1)} reshape(bf16[8,2,32768]{2,1,0:T(2,128)(2,1)S(1)} %all-to-all-done.3) | data formatting | bytes 2097152
  394.1 9.1 %copy.29 = bf16[16,256,8,16]{1,3,2,0:T(8,128)(2,1)} copy(bf16[16,256,8,16]{3,0,1,2:T(8,128)(2,1)} %bitcast.72) | data formatting | bytes 2097152 | tf_op jit(solution)/shard_map/all_to_all | solution.py:68
  403.2 7.6 %reshape.112 = bf16[2048,16,16]{2,1,0:T(8,128)(2,1)} reshape(bf16[8,2,32768]{2,1,0:T(2,128)(2,1)S(1)} %all-to-all-done.1) | data formatting | bytes 2097152
  410.8 9.1 %copy.26 = bf16[16,256,8,16]{1,3,2,0:T(8,128)(2,1)} copy(bf16[16,256,8,16]{3,0,1,2:T(8,128)(2,1)} %bitcast.73) | data formatting | bytes 2097152 | tf_op jit(solution)/shard_map/all_to_all | solution.py:68
  (71 shorter events, 39.6 us)
Async XLA Ops:
  7.2 263.8 %copy-start = (bf16[256,2048]{1,0:T(8,128)(2,1)S(1)}, bf16[256,2048]{1,0:T(8,128)(2,1)}, u32[]{:S(2)}) copy-start(bf16[256,2048]{1,0:T(8,128)(2,1)} %param.16) | copy-start | bytes 3145732
  7.2 4.8 %copy-start.14 = (s32[1,2]{1,0:T(1,128)S(1)}, s32[1,2]{1,0:T(1,128)}, u32[]{:S(2)}) copy-start(s32[1,2]{1,0:T(1,128)} %param.13) | copy-start | bytes 28
  7.2 10.7 %copy-start.11 = (bf16[1,2048]{1,0:T(2,128)(2,1)S(1)}, bf16[1,2048]{1,0:T(2,128)(2,1)}, u32[]{:S(2)}) copy-start(bf16[1,2048]{1,0:T(2,128)(2,1)} %param.15) | copy-start | bytes 12292
  7.2 40.6 %all-gather.6.cloned.1.call-start = ((), (), s32[]{:S(2)}) async-start(), calls=%async_computation.4 | async-start | bytes 5242880 | tf_op jit(solution)/shard_map/all_gather | solution.py:44
  10.5 164.4 %all-gather.10.cloned.1.call-start = ((), (), s32[]{:S(2)}) async-start(), calls=%async_computation.6 | async-start | bytes 9437184 | tf_op jit(solution)/shard_map/all_gather | solution.py:35
  11.2 206.8 %all-gather.8.cloned.1.call-start = ((), (), s32[]{:S(2)}) async-start(), calls=%async_computation.5 | async-start | bytes 5242880 | tf_op jit(solution)/shard_map/all_gather | solution.py:44
  190.7 61.9 %all-to-all-start = ((bf16[4,256,2048]{2,1,0:T(8,128)(2,1)}), bf16[4,256,2048]{2,1,0:T(8,128)(2,1)}, u32[]{:S(2)}, u32[]{:S(2)}) async-start(bf16[4,256,2048]{2,1,0:T(8,128)(2,1)} %multiply_convert_fusion.1), calls=%async_computation | async-start | bytes 8388608 | tf_op jit(solution)/shard_map/all_to_all | solution.py:51
  218.0 3.4 copy-start.7
  235.9 21.7 %copy-start.10 = (s32[1,2,2,16,16]{4,3,2,1,0:T(8,128)S(1)}, s32[1,2,2,16,16]{4,3,2,1,0:T(8,128)}, u32[]{:S(2)}) copy-start(s32[1,2,2,16,16]{4,3,2,1,0:T(8,128)} %param.12) | copy-start | bytes 12292
  235.9 21.9 %copy-start.4 = (bf16[1,2,16,16,2048]{4,3,2,1,0:T(8,128)(2,1)S(1)}, bf16[1,2,16,16,2048]{4,3,2,1,0:T(8,128)(2,1)}, u32[]{:S(2)}) copy-start(bf16[1,2,16,16,2048]{4,3,2,1,0:T(8,128)(2,1)} %param.10) | copy-start | bytes 6291460
  235.9 22.4 %copy-start.12 = (bf16[2048]{0:T(1024)(128)(2,1)S(1)}, bf16[2048]{0:T(1024)(128)(2,1)}, u32[]{:S(2)}) copy-start(bf16[2048]{0:T(1024)(128)(2,1)} %param.17) | copy-start | bytes 12292
  252.6 53.1 %all-to-all-start.2 = ((bf16[4,256,2048]{2,1,0:T(8,128)(2,1)}), bf16[4,256,2048]{2,1,0:T(8,128)(2,1)}, u32[]{:S(2)}, u32[]{:S(2)}) async-start(bf16[4,256,2048]{2,1,0:T(8,128)(2,1)} %multiply_convert_fusion), calls=%async_computation.2 | async-start | bytes 8388608 | tf_op jit(solution)/shard_map/all_to_all | solution.py:51
  266.1 4.9 %copy-start.5 = (f32[512,2048]{1,0:T(8,128)}, f32[512,2048]{1,0:T(8,128)S(1)}, u32[]{:S(2)}) copy-start(f32[512,2048]{1,0:T(8,128)S(1)} %bitcast_add_fusion) | copy-start | bytes 12582916
  266.1 4.9 %copy-start.2 = (bf16[1,1,16,16,2048]{4,3,2,1,0:T(8,128)(2,1)S(1)}, bf16[1,1,16,16,2048]{4,3,2,1,0:T(8,128)(2,1)}, u32[]{:S(2)}) copy-start(bf16[1,1,16,16,2048]{4,3,2,1,0:T(8,128)(2,1)} %get-tuple-element.8) | copy-start | bytes 3145732
  273.1 36.0 %copy-start.1 = (bf16[1,1,16,16,2048]{4,3,2,1,0:T(8,128)(2,1)S(1)}, bf16[1,1,16,16,2048]{4,3,2,1,0:T(8,128)(2,1)}, u32[]{:S(2)}) copy-start(bf16[1,1,16,16,2048]{4,3,2,1,0:T(8,128)(2,1)} %get-tuple-element.9) | copy-start | bytes 3145732
  305.7 3.4 copy-start.6
  309.1 1.6 copy-start.3
  311.1 8.8 %copy-start.9 = (bf16[256,2048]{1,0:T(8,128)(2,1)}, bf16[256,2048]{1,0:T(8,128)(2,1)S(1)}, u32[]{:S(2)}) copy-start(bf16[256,2048]{1,0:T(8,128)(2,1)S(1)} %get-tuple-element.15) | copy-start | bytes 3145732
  311.2 33.1 %copy-start.8 = (bf16[256,2048]{1,0:T(8,128)(2,1)}, bf16[256,2048]{1,0:T(8,128)(2,1)S(1)}, u32[]{:S(2)}) copy-start(bf16[256,2048]{1,0:T(8,128)(2,1)S(1)} %get-tuple-element.14) | copy-start | bytes 3145732
  338.7 33.1 %all-to-all-start.3 = ((bf16[8,2,32768]{2,1,0:T(2,128)(2,1)}), bf16[8,2,32768]{2,1,0:T(2,128)(2,1)S(1)}, u32[]{:S(2)}, u32[]{:S(2)}) async-start(bf16[8,2,32768]{2,1,0:T(2,128)(2,1)} %reshape.109), calls=%async_computation.3 | async-start | bytes 2097152 | tf_op jit(solution)/shard_map/all_to_all | solution.py:68
  360.5 17.2 %copy-start.13 = (bf16[1024]{0:T(1024)(128)(2,1)S(1)}, bf16[1024]{0:T(1024)(128)(2,1)}, u32[]{:S(2)}) copy-start(bf16[1024]{0:T(1024)(128)(2,1)} %param.19) | copy-start | bytes 6148
  371.8 31.4 %all-to-all-start.1 = ((bf16[8,2,32768]{2,1,0:T(2,128)(2,1)}), bf16[8,2,32768]{2,1,0:T(2,128)(2,1)S(1)}, u32[]{:S(2)}, u32[]{:S(2)}) async-start(bf16[8,2,32768]{2,1,0:T(2,128)(2,1)} %reshape.111), calls=%async_computation.1 | async-start | bytes 2097152 | tf_op jit(solution)/shard_map/all_to_all | solution.py:68
Sparse Core Ops, SparseCore 0:
  10.6 37.1 all-gather.5
  49.9 124.9 all-gather.9
  176.5 41.4 all-gather.7
where the time goes:
time: 432 us; the launch traced here: 431 us
  waiting for transfers between devices  227 us (53%)
  local copies, waits for them, and re-layouts  95.7 us (22%)
  matrix products  41.7 us (10%)
  other arithmetic  24.9 us (6%)
  starting transfers between devices  21.6 us (5%)
  between operations  14 us (3%)
  blocking collectives  5.95 us (1%)
    all_gather x1, waiting for transfers between devices, local(): own_whole = lax.all_gather(weight_shard, 'env', axis=0, tiled=True)  124 us
    unnamed x38, local copies, waits for them, and re-layouts  56 us
    all_gather x2, waiting for transfers between devices, local(): all_rows = lax.all_gather(opp_raw, 'league', axis=0, tiled=True)  52.1 us
    all_to_all x2, waiting for transfers between devices, local(): lax.all_to_all(products, 'league', split_axis=0, concat_axis=0, tiled=True)  49.2 us
    dot_general x2, matrix products, local(): jnp.dot(all_normed, own_whole, preferred_element_type=jnp.float32)  23.9 us
    all_to_all x2, local copies, waits for them, and re-layouts, local(): lax.all_to_all(time_block, 'env', split_axis=1, concat_axis=2, tiled=True)  18.2 us
    reshape x2, local copies, waits for them, and re-layouts, local(): joint_row.reshape(env_count, step_count, model_width).transpose(1, 2, 0)  17.7 us
    all_to_all x2, starting transfers between devices, local(): lax.all_to_all(time_block, 'env', split_axis=1, concat_axis=2, tiled=True)  11.5 us
  transfers between devices with their start and end apart: 7, of which 5 were waited for; matrix products, arithmetic and copies ran while one was open for 24% of the time, Pallas kernels for 0%

commit v1 on v0

--- a/solution.py
+++ b/solution.py
@@ -65,7 +65,27 @@
         value_est = jnp.dot(value_hidden, value_out, preferred_element_type=jnp.float32)
         value_list.append(value_est.reshape(env_count, step_count))
         time_block = joint_row.reshape(env_count, step_count, model_width).transpose(1, 2, 0)
-        traj_list.append(lax.all_to_all(time_block, "env", split_axis=1, concat_axis=2, tiled=True))
+
+        def assign_slot(x_part):
+            x_now, e_now = (lax.axis_size("env"), lax.axis_index("env"))
+            f_next = x_part.shape[1] // x_now
+            seen_now = list(x_part.shape)
+            seen_now[1] = f_next
+            high = seen_now[2]
+            seen_now[2] = high * x_now
+            y = jnp.zeros(seen_now, x_part.dtype)
+            w = 0
+            while w < x_now:
+                arr_now = lax.dynamic_slice_in_dim(x_part, (e_now ^ w) * f_next, f_next, axis=1)
+                if w:
+                    arr_now = lax.ppermute(
+                        arr_now, "env", [(src_i, src_i ^ w) for src_i in range(x_now)]
+                    )
+                y = lax.dynamic_update_slice_in_dim(y, arr_now, (e_now ^ w) * high, axis=2)
+                w += 1
+            return y
+
+        traj_list.append(assign_slot(time_block))
     learner_rows = jnp.stack(traj_list)
     values = jnp.stack(value_list)
     return (learner_rows[None], values[None])

time: 432 us -> 584 us (1.35)
  local copies, waits for them, and re-layouts: 95.7 us -> 227 us
  starting transfers between devices: 21.6 us -> 37.5 us
    dynamic_update_slice x0 -> x16, local copies, waits for them, and re-layouts: none -> 179 us  [assign_slot(): y = lax.dynamic_update_slice_in_dim(y, arr_now, (e_now ^ w) * high, axis=2)]
    unnamed x38 -> x47, local copies, waits for them, and re-layouts: 56 us -> 12.8 us
    another operation x0 -> x18, local copies, waits for them, and re-layouts: none -> 31.3 us  [the longest x16 30.2 us: local(): learner_rows = jnp.stack(traj_list)]
    ppermute x0 -> x14, starting transfers between devices: none -> 27.5 us  [assign_slot(): lax.ppermute(arr_now, 'env', [(src_i, src_i ^ w) for src_i in range(x_now)])]
    all_to_all x2 -> x0, local copies, waits for them, and re-layouts: 18.2 us -> none  [local(): lax.all_to_all(time_block, 'env', split_axis=1, concat_axis=2, tiled=True)]
    reshape x2 -> x0, local copies, waits for them, and re-layouts: 17.7 us -> none  [local(): joint_row.reshape(env_count, step_count, model_width).transpose(1, 2, 0)]
    all_to_all x2 -> x0, starting transfers between devices: 11.5 us -> none  [local(): lax.all_to_all(time_block, 'env', split_axis=1, concat_axis=2, tiled=True)]
  transfers between devices with their start and end apart: 7 -> 19, of which waited for: 5 -> 5; matrix products, arithmetic and copies ran while one was open for 24% -> 20% of each run, Pallas kernels for 0% -> 0%
where the time goes in v1:
time: 584 us; the launch traced here: 579 us
  local copies, waits for them, and re-layouts  227 us (39%)
  waiting for transfers between devices  227 us (39%)
  matrix products  41 us (7%)
  starting transfers between devices  37.5 us (6%)
  other arithmetic  26.2 us (4%)
  between operations  14.2 us (2%)
  blocking collectives  5.95 us (1%)
    dynamic_update_slice x16, local copies, waits for them, and re-layouts, assign_slot(): y = lax.dynamic_update_slice_in_dim(y, arr_now, (e_now ^ w) * high, axis=2)  179 us
    all_gather x1, waiting for transfers between devices, local(): own_whole = lax.all_gather(weight_shard, 'env', axis=0, tiled=True)  124 us
    all_gather x2, waiting for transfers between devices, local(): all_rows = lax.all_gather(opp_raw, 'league', axis=0, tiled=True)  52.1 us
    all_to_all x2, waiting for transfers between devices, local(): lax.all_to_all(products, 'league', split_axis=0, concat_axis=0, tiled=True)  49.1 us
    another operation x16, local copies, waits for them, and re-layouts, local(): learner_rows = jnp.stack(traj_list)  30.2 us
    ppermute x14, starting transfers between devices, assign_slot(): lax.ppermute(arr_now, 'env', [(src_i, src_i ^ w) for src_i in range(x_now)])  27.5 us
    dot_general x2, matrix products, local(): jnp.dot(all_normed, own_whole, preferred_element_type=jnp.float32)  23.9 us
    unnamed x47, local copies, waits for them, and re-layouts  12.8 us
  transfers between devices with their start and end apart: 19, of which 5 were waited for; matrix products, arithmetic and copies ran while one was open for 20% of the time, Pallas kernels for 0%

profile of v1, /device:TPU:0, one launch (start us, length us, event | category | flops | bytes accessed | tf_op | source)
XLA Modules:
  0.0 578.6 jit_solution(15126745250628249159)
XLA Ops:
  11.9 6.0 %all-gather.1 = s32[4,1,2]{2,1,0:T(1,128)S(1)} all-gather(s32[1,1,2]{2,1,0:T(1,128)S(1)} %bitcast.135), channel_id=1, replica_groups=mesh['league'=4,'env'=8] {'league'}, dimensions={0}, use_global_device_ids=true | all-gather | bytes 40 | tf_op jit(solution)/shard_map/all_gather | solution.py:37
  18.0 29.8 %all-gather.8.cloned.1.call-done = bf16[1024,2048]{1,0:T(8,128)(2,1)} async-done(((bf16[256,2048]{1,0:T(8,128)(2,1)}), bf16[1024,2048]{1,0:T(8,128)(2,1)}) %all-gather.8.cloned.1.call-update) | async-done | bytes 4194320 | tf_op jit(solution)/shard_map/all_gather | solution.py:44
  50.9 124.0 %all-gather.10.cloned.1.call-done = bf16[1,2048,2048]{2,1,0:T(8,128)(2,1)} async-done(((bf16[1,256,2048]{2,1,0:T(8,128)(2,1)}), bf16[1,2048,2048]{2,1,0:T(8,128)(2,1)}) %all-gather.10.cloned.1.call-update) | async-done | bytes 8388624 | tf_op jit(solution)/shard_map/all_gather | solution.py:35
  174.9 12.6 %fusion.6 = f32[1024,2048]{1,0:T(8,128)S(1)} fusion(bf16[1,2048,2048]{2,1,0:T(8,128)(2,1)} %all-gather.10.cloned.1.call-done, bf16[1024,2048]{1,0:T(8,128)(2,1)} %all-gather.8.cloned.1.call-done, f32[1024]{0:T(1024)S(1)} %add_rsqrt_fusion.1, f32[2048]{0:T(1024)S(1)} %bitcast.129), kind=kOutput, calls=%fused_computation.10 | convolution fusion | flops 8598323200 | bytes 20983808 | tf_op jit(solution)/shard_map/dot_general | solution.py:46
  195.6 22.3 %all-gather.6.cloned.1.call-done = bf16[1024,2048]{1,0:T(8,128)(2,1)} async-done(((bf16[256,2048]{1,0:T(8,128)(2,1)}), bf16[1024,2048]{1,0:T(8,128)(2,1)}) %all-gather.6.cloned.1.call-update) | async-done | bytes 4194320 | tf_op jit(solution)/shard_map/all_gather | solution.py:44
  221.4 11.3 %fusion.8 = f32[1024,2048]{1,0:T(8,128)S(1)} fusion(bf16[1,2048,2048]{2,1,0:T(8,128)(2,1)} %all-gather.10.cloned.1.call-done, bf16[1024,2048]{1,0:T(8,128)(2,1)S(1)} %copy-done.8, f32[2048]{0:T(1024)S(1)} %bitcast.130, f32[1024]{0:T(1024)S(1)} %add_rsqrt_fusion.2), kind=kOutput, calls=%fused_computation.12 | convolution fusion | flops 8598323200 | bytes 20983808 | tf_op jit(solution)/shard_map/dot_general | solution.py:46
  236.0 16.6 %all-to-all-done.1 = bf16[4,256,2048]{2,1,0:T(8,128)(2,1)} async-done(((bf16[4,256,2048]{2,1,0:T(8,128)(2,1)}), bf16[4,256,2048]{2,1,0:T(8,128)(2,1)}, u32[]{:S(2)}, u32[]{:S(2)}) %all-to-all-start.1) | async-done | bytes 4194336 | tf_op jit(solution)/shard_map/all_to_all | solution.py:51
  259.2 7.0 %bitcast_add_fusion = f32[512,2048]{1,0:T(8,128)S(1)} fusion(bf16[1,2,16,16,2048]{4,3,2,1,0:T(8,128)(2,1)S(1)} %copy-done.4, bf16[512,2048]{1,0:T(8,128)(2,1)S(1)} %fusion.16, bf16[1,2048,2048]{2,1,0:T(8,128)(2,1)} %all-gather.10.cloned.1.call-done), kind=kOutput, calls=%fused_computation.20 | convolution fusion | flops 4297064448 | bytes 16777216 | tf_op jit(solution)/shard_map/dot_general | solution.py:36
  273.2 32.5 %all-to-all-done = bf16[4,256,2048]{2,1,0:T(8,128)(2,1)} async-done(((bf16[4,256,2048]{2,1,0:T(8,128)(2,1)}), bf16[4,256,2048]{2,1,0:T(8,128)(2,1)}, u32[]{:S(2)}, u32[]{:S(2)}) %all-to-all-start) | async-done | bytes 4194336 | tf_op jit(solution)/shard_map/all_to_all | solution.py:51
  360.0 9.2 %dynamic_update_slice.64 = bf16[1,16,256,128]{3,2,1,0:T(8,128)(2,1)} dynamic-update-slice(bf16[1,16,256,128]{3,2,1,0:T(8,128)(2,1)} %stack.42.clone.1, bf16[1,16,256,16]{3,2,1,0:T(8,128)(2,1)S(1)} %bitcast.121, s32[]{:T(128)} %constant.55.clone.1, s32[]{:T(128)} %constant.55.clone.1, s32[]{:T(128)} %constant.55.clone.1, s32[]{:T(128)S(6)} %select_n.65) | dynamic-update-slice | bytes 262148 | tf_op jit(solution)/shard_map/dynamic_update_slice | solution.py:84
  402.7 12.0 %dynamic_update_slice.65 = bf16[1,16,256,128]{3,2,1,0:T(8,128)(2,1)} dynamic-update-slice(bf16[1,16,256,128]{3,2,1,0:T(8,128)(2,1)} %dynamic_update_slice.64, bf16[1,16,256,16]{3,2,1,0:T(8,128)(2,1)} %copy.32, s32[]{:T(128)} %constant.55.clone.1, s32[]{:T(128)} %constant.55.clone.1, s32[]{:T(128)} %constant.55.clone.1, s32[]{:T(128)S(6)} %select_n.67) | dynamic-update-slice | bytes 262148 | tf_op jit(solution)/shard_map/dynamic_update_slice | solution.py:84
  414.7 12.0 %dynamic_update_slice.73 = bf16[1,16,256,128]{3,2,1,0:T(8,128)(2,1)} dynamic-update-slice(bf16[1,16,256,128]{3,2,1,0:T(8,128)(2,1)} %copy-done.9, bf16[1,16,256,16]{3,2,1,0:T(8,128)(2,1)} %copy.47, s32[]{:T(128)} %constant.55.clone.1, s32[]{:T(128)} %constant.55.clone.1, s32[]{:T(128)} %constant.55.clone.1, s32[]{:T(128)S(6)} %select_n.67) | dynamic-update-slice | bytes 262148 | tf_op jit(solution)/shard_map/dynamic_update_slice | solution.py:84
  426.7 12.0 %dynamic_update_slice.66 = bf16[1,16,256,128]{3,2,1,0:T(8,128)(2,1)} dynamic-update-slice(bf16[1,16,256,128]{3,2,1,0:T(8,128)(2,1)} %dynamic_update_slice.65, bf16[1,16,256,16]{3,2,1,0:T(8,128)(2,1)} %copy.34, s32[]{:T(128)} %constant.55.clone.1, s32[]{:T(128)} %constant.55.clone.1, s32[]{:T(128)} %constant.55.clone.1, s32[]{:T(128)S(6)} %select_n.69) | dynamic-update-slice | bytes 262148 | tf_op jit(solution)/shard_map/dynamic_update_slice | solution.py:84
  438.7 12.0 %dynamic_update_slice.74 = bf16[1,16,256,128]{3,2,1,0:T(8,128)(2,1)} dynamic-update-slice(bf16[1,16,256,128]{3,2,1,0:T(8,128)(2,1)} %dynamic_update_slice.73, bf16[1,16,256,16]{3,2,1,0:T(8,128)(2,1)} %copy.49, s32[]{:T(128)} %constant.55.clone.1, s32[]{:T(128)} %constant.55.clone.1, s32[]{:T(128)} %constant.55.clone.1, s32[]{:T(128)S(6)} %select_n.69) | dynamic-update-slice | bytes 262148 | tf_op jit(solution)/shard_map/dynamic_update_slice | solution.py:84
  450.7 12.0 %dynamic_update_slice.67 = bf16[1,16,256,128]{3,2,1,0:T(8,128)(2,1)} dynamic-update-slice(bf16[1,16,256,128]{3,2,1,0:T(8,128)(2,1)} %dynamic_update_slice.66, bf16[1,16,256,16]{3,2,1,0:T(8,128)(2,1)} %copy.36, s32[]{:T(128)} %constant.55.clone.1, s32[]{:T(128)} %constant.55.clone.1, s32[]{:T(128)} %constant.55.clone.1, s32[]{:T(128)S(6)} %select_n.71) | dynamic-update-slice | bytes 262148 | tf_op jit(solution)/shard_map/dynamic_update_slice | solution.py:84
  462.7 12.0 %dynamic_update_slice.75 = bf16[1,16,256,128]{3,2,1,0:T(8,128)(2,1)} dynamic-update-slice(bf16[1,16,256,128]{3,2,1,0:T(8,128)(2,1)} %dynamic_update_slice.74, bf16[1,16,256,16]{3,2,1,0:T(8,128)(2,1)} %copy.51, s32[]{:T(128)} %constant.55.clone.1, s32[]{:T(128)} %constant.55.clone.1, s32[]{:T(128)} %constant.55.clone.1, s32[]{:T(128)S(6)} %select_n.71) | dynamic-update-slice | bytes 262148 | tf_op jit(solution)/shard_map/dynamic_update_slice | solution.py:84
  474.7 12.0 %dynamic_update_slice.68 = bf16[1,16,256,128]{3,2,1,0:T(8,128)(2,1)} dynamic-update-slice(bf16[1,16,256,128]{3,2,1,0:T(8,128)(2,1)} %dynamic_update_slice.67, bf16[1,16,256,16]{3,2,1,0:T(8,128)(2,1)} %copy.38, s32[]{:T(128)} %constant.55.clone.1, s32[]{:T(128)} %constant.55.clone.1, s32[]{:T(128)} %constant.55.clone.1, s32[]{:T(128)S(6)} %select_n.73) | dynamic-update-slice | bytes 262148 | tf_op jit(solution)/shard_map/dynamic_update_slice | solution.py:84
  486.7 12.0 %dynamic_update_slice.76 = bf16[1,16,256,128]{3,2,1,0:T(8,128)(2,1)} dynamic-update-slice(bf16[1,16,256,128]{3,2,1,0:T(8,128)(2,1)} %dynamic_update_slice.75, bf16[1,16,256,16]{3,2,1,0:T(8,128)(2,1)} %copy.53, s32[]{:T(128)} %constant.55.clone.1, s32[]{:T(128)} %constant.55.clone.1, s32[]{:T(128)} %constant.55.clone.1, s32[]{:T(128)S(6)} %select_n.73) | dynamic-update-slice | bytes 262148 | tf_op jit(solution)/shard_map/dynamic_update_slice | solution.py:84
  498.7 12.0 %dynamic_update_slice.69 = bf16[1,16,256,128]{3,2,1,0:T(8,128)(2,1)} dynamic-update-slice(bf16[1,16,256,128]{3,2,1,0:T(8,128)(2,1)} %dynamic_update_slice.68, bf16[1,16,256,16]{3,2,1,0:T(8,128)(2,1)} %copy.40, s32[]{:T(128)} %constant.55.clone.1, s32[]{:T(128)} %constant.55.clone.1, s32[]{:T(128)} %constant.55.clone.1, s32[]{:T(128)S(6)} %select_n.75) | dynamic-update-slice | bytes 262148 | tf_op jit(solution)/shard_map/dynamic_update_slice | solution.py:84
  510.7 12.0 %dynamic_update_slice.77 = bf16[1,16,256,128]{3,2,1,0:T(8,128)(2,1)} dynamic-update-slice(bf16[1,16,256,128]{3,2,1,0:T(8,128)(2,1)} %dynamic_update_slice.76, bf16[1,16,256,16]{3,2,1,0:T(8,128)(2,1)} %copy.55, s32[]{:T(128)} %constant.55.clone.1, s32[]{:T(128)} %constant.55.clone.1, s32[]{:T(128)} %constant.55.clone.1, s32[]{:T(128)S(6)} %select_n.75) | dynamic-update-slice | bytes 262148 | tf_op jit(solution)/shard_map/dynamic_update_slice | solution.py:84
  522.7 11.4 %dynamic_update_slice.70 = bf16[1,16,256,128]{3,2,1,0:T(8,128)(2,1)} dynamic-update-slice(bf16[1,16,256,128]{3,2,1,0:T(8,128)(2,1)} %dynamic_update_slice.69, bf16[1,16,256,16]{3,2,1,0:T(8,128)(2,1)S(1)} %copy.42, s32[]{:T(128)} %constant.55.clone.1, s32[]{:T(128)} %constant.55.clone.1, s32[]{:T(128)} %constant.55.clone.1, s32[]{:T(128)S(6)} %select_n.77) | dynamic-update-slice | bytes 262148 | tf_op jit(solution)/shard_map/dynamic_update_slice | solution.py:84
  534.1 12.1 %dynamic_update_slice.78 = bf16[1,16,256,128]{3,2,1,0:T(8,128)(2,1)} dynamic-update-slice(bf16[1,16,256,128]{3,2,1,0:T(8,128)(2,1)} %dynamic_update_slice.77, bf16[1,16,256,16]{3,2,1,0:T(8,128)(2,1)} %copy.57, s32[]{:T(128)} %constant.55.clone.1, s32[]{:T(128)} %constant.55.clone.1, s32[]{:T(128)} %constant.55.clone.1, s32[]{:T(128)S(6)} %select_n.77) | dynamic-update-slice | bytes 262148 | tf_op jit(solution)/shard_map/dynamic_update_slice | solution.py:84
  546.2 11.4 %dynamic_update_slice.71 = bf16[1,16,256,128]{3,2,1,0:T(8,128)(2,1)} dynamic-update-slice(bf16[1,16,256,128]{3,2,1,0:T(8,128)(2,1)} %dynamic_update_slice.70, bf16[1,16,256,16]{3,2,1,0:T(8,128)(2,1)S(1)} %copy.44, s32[]{:T(128)} %constant.55.clone.1, s32[]{:T(128)} %constant.55.clone.1, s32[]{:T(128)} %constant.55.clone.1, s32[]{:T(128)S(6)} %select_n.79) | dynamic-update-slice | bytes 262148 | tf_op jit(solution)/shard_map/dynamic_update_slice | solution.py:84
  557.6 11.4 %dynamic_update_slice.79 = bf16[1,16,256,128]{3,2,1,0:T(8,128)(2,1)} dynamic-update-slice(bf16[1,16,256,128]{3,2,1,0:T(8,128)(2,1)} %dynamic_update_slice.78, bf16[1,16,256,16]{3,2,1,0:T(8,128)(2,1)S(1)} %copy-done.7, s32[]{:T(128)} %constant.55.clone.1, s32[]{:T(128)} %constant.55.clone.1, s32[]{:T(128)} %constant.55.clone.1, s32[]{:T(128)S(6)} %select_n.79) | dynamic-update-slice | bytes 262148 | tf_op jit(solution)/shard_map/dynamic_update_slice | solution.py:84
  (134 shorter events, 126.9 us)
Async XLA Ops:
  7.2 263.9 %copy-start = (bf16[256,2048]{1,0:T(8,128)(2,1)S(1)}, bf16[256,2048]{1,0:T(8,128)(2,1)}, u32[]{:S(2)}) copy-start(bf16[256,2048]{1,0:T(8,128)(2,1)} %param.16) | copy-start | bytes 3145732
  7.2 40.6 %all-gather.8.cloned.1.call-start = ((), (), s32[]{:S(2)}) async-start(), calls=%async_computation.3 | async-start | bytes 5242880 | tf_op jit(solution)/shard_map/all_gather | solution.py:44
  10.5 164.4 %all-gather.10.cloned.1.call-start = ((), (), s32[]{:S(2)}) async-start(), calls=%async_computation.4 | async-start | bytes 9437184 | tf_op jit(solution)/shard_map/all_gather | solution.py:35
  11.2 206.7 %all-gather.6.cloned.1.call-start = ((), (), s32[]{:S(2)}) async-start(), calls=%async_computation.2 | async-start | bytes 5242880 | tf_op jit(solution)/shard_map/all_gather | solution.py:44
  190.7 61.9 %all-to-all-start.1 = ((bf16[4,256,2048]{2,1,0:T(8,128)(2,1)}), bf16[4,256,2048]{2,1,0:T(8,128)(2,1)}, u32[]{:S(2)}, u32[]{:S(2)}) async-start(bf16[4,256,2048]{2,1,0:T(8,128)(2,1)} %multiply_convert_fusion), calls=%async_computation.1 | async-start | bytes 8388608 | tf_op jit(solution)/shard_map/all_to_all | solution.py:51
  236.0 22.6 %copy-start.12 = (bf16[2048]{0:T(1024)(128)(2,1)S(1)}, bf16[2048]{0:T(1024)(128)(2,1)}, u32[]{:S(2)}) copy-start(bf16[2048]{0:T(1024)(128)(2,1)} %param.17) | copy-start | bytes 12292
  236.0 22.6 %copy-start.13 = (bf16[1024]{0:T(1024)(128)(2,1)S(1)}, bf16[1024]{0:T(1024)(128)(2,1)}, u32[]{:S(2)}) copy-start(bf16[1024]{0:T(1024)(128)(2,1)} %param.19) | copy-start | bytes 6148
  252.6 53.1 %all-to-all-start = ((bf16[4,256,2048]{2,1,0:T(8,128)(2,1)}), bf16[4,256,2048]{2,1,0:T(8,128)(2,1)}, u32[]{:S(2)}, u32[]{:S(2)}) async-start(bf16[4,256,2048]{2,1,0:T(8,128)(2,1)} %multiply_convert_fusion.1), calls=%async_computation | async-start | bytes 8388608 | tf_op jit(solution)/shard_map/all_to_all | solution.py:51
  273.2 35.9 %copy-start.1 = (bf16[1,1,16,16,2048]{4,3,2,1,0:T(8,128)(2,1)S(1)}, bf16[1,1,16,16,2048]{4,3,2,1,0:T(8,128)(2,1)}, u32[]{:S(2)}) copy-start(bf16[1,1,16,16,2048]{4,3,2,1,0:T(8,128)(2,1)} %get-tuple-element.2) | copy-start | bytes 3145732
  311.4 12.1 %collective-permute-start = (bf16[16,256,16]{1,2,0:T(8,128)(2,1)S(1)}, bf16[16,256,16]{1,2,0:T(8,128)(2,1)}, u32[]{:S(2)}, u32[]{:S(2)}) collective-permute-start(bf16[16,256,16]{1,2,0:T(8,128)(2,1)S(1)} %bitcast.128), channel_id=1, source_target_pairs={{0,1},{1,0},{2,3},{3,2},{4,5},{5,4},{6,7},{7,6},{8,9},{9,8},{10,11... | collective-permute-start | bytes 393224 | tf_op jit(solution)/shard_map/ppermute | solution.py:81
  312.9 13.8 %collective-permute-start.1 = (bf16[16,256,16]{1,2,0:T(8,128)(2,1)S(1)}, bf16[16,256,16]{1,2,0:T(8,128)(2,1)}, u32[]{:S(2)}, u32[]{:S(2)}) collective-permute-start(bf16[16,256,16]{1,2,0:T(8,128)(2,1)S(1)} %bitcast.127), channel_id=1, source_target_pairs={{0,2},{1,3},{2,0},{3,1},{4,6},{5,7},{6,4},{7,5},{8,10},{9,11},{10,... | collective-permute-start | bytes 393224 | tf_op jit(solution)/shard_map/ppermute | solution.py:81
  314.5 12.7 %collective-permute-start.2 = (bf16[16,256,16]{1,2,0:T(8,128)(2,1)S(1)}, bf16[16,256,16]{1,2,0:T(8,128)(2,1)}, u32[]{:S(2)}, u32[]{:S(2)}) collective-permute-start(bf16[16,256,16]{1,2,0:T(8,128)(2,1)S(1)} %bitcast.126), channel_id=1, source_target_pairs={{0,3},{1,2},{2,1},{3,0},{4,7},{5,6},{6,5},{7,4},{8,11},{9,10},{10,... | collective-permute-start | bytes 393224 | tf_op jit(solution)/shard_map/ppermute | solution.py:81
  315.2 13.5 %collective-permute-start.3 = (bf16[16,256,16]{1,2,0:T(8,128)(2,1)S(1)}, bf16[16,256,16]{1,2,0:T(8,128)(2,1)}, u32[]{:S(2)}, u32[]{:S(2)}) collective-permute-start(bf16[16,256,16]{1,2,0:T(8,128)(2,1)S(1)} %bitcast.125), channel_id=1, source_target_pairs={{0,4},{1,5},{2,6},{3,7},{4,0},{5,1},{6,2},{7,3},{8,12},{9,13},{10,... | collective-permute-start | bytes 393224 | tf_op jit(solution)/shard_map/ppermute | solution.py:81
  318.3 24.7 %collective-permute-start.4 = (bf16[16,256,16]{1,2,0:T(8,128)(2,1)}, bf16[16,256,16]{1,2,0:T(8,128)(2,1)}, u32[]{:S(2)}, u32[]{:S(2)}) collective-permute-start(bf16[16,256,16]{1,2,0:T(8,128)(2,1)} %bitcast.109), channel_id=1, source_target_pairs={{0,5},{1,4},{2,7},{3,6},{4,1},{5,0},{6,3},{7,2},{8,13},{9,12},{10,... | collective-permute-start | bytes 393224 | tf_op jit(solution)/shard_map/ppermute | solution.py:81
  323.4 21.6 %collective-permute-start.5 = (bf16[16,256,16]{1,2,0:T(8,128)(2,1)}, bf16[16,256,16]{1,2,0:T(8,128)(2,1)}, u32[]{:S(2)}, u32[]{:S(2)}) collective-permute-start(bf16[16,256,16]{1,2,0:T(8,128)(2,1)} %bitcast.108), channel_id=1, source_target_pairs={{0,6},{1,7},{2,4},{3,5},{4,2},{5,3},{6,0},{7,1},{8,14},{9,15},{10,... | collective-permute-start | bytes 393224 | tf_op jit(solution)/shard_map/ppermute | solution.py:81
  326.7 21.9 %collective-permute-start.6 = (bf16[16,256,16]{1,2,0:T(8,128)(2,1)}, bf16[16,256,16]{1,2,0:T(8,128)(2,1)}, u32[]{:S(2)}, u32[]{:S(2)}) collective-permute-start(bf16[16,256,16]{1,2,0:T(8,128)(2,1)} %bitcast.107), channel_id=1, source_target_pairs={{0,7},{1,6},{2,5},{3,4},{4,3},{5,2},{6,1},{7,0},{8,15},{9,14},{10,... | collective-permute-start | bytes 393224 | tf_op jit(solution)/shard_map/ppermute | solution.py:81
  327.2 21.9 %collective-permute-start.7 = (bf16[16,256,16]{1,2,0:T(8,128)(2,1)}, bf16[16,256,16]{1,2,0:T(8,128)(2,1)}, u32[]{:S(2)}, u32[]{:S(2)}) collective-permute-start(bf16[16,256,16]{1,2,0:T(8,128)(2,1)} %bitcast.106), channel_id=1, source_target_pairs={{0,1},{1,0},{2,3},{3,2},{4,5},{5,4},{6,7},{7,6},{8,9},{9,8},{10,11... | collective-permute-start | bytes 393224 | tf_op jit(solution)/shard_map/ppermute | solution.py:81
  328.7 24.7 %collective-permute-start.8 = (bf16[16,256,16]{1,2,0:T(8,128)(2,1)}, bf16[16,256,16]{1,2,0:T(8,128)(2,1)}, u32[]{:S(2)}, u32[]{:S(2)}) collective-permute-start(bf16[16,256,16]{1,2,0:T(8,128)(2,1)} %bitcast.105), channel_id=1, source_target_pairs={{0,2},{1,3},{2,0},{3,1},{4,6},{5,7},{6,4},{7,5},{8,10},{9,11},{10,... | collective-permute-start | bytes 393224 | tf_op jit(solution)/shard_map/ppermute | solution.py:81
  343.1 49.4 %collective-permute-start.9 = (bf16[16,256,16]{1,2,0:T(8,128)(2,1)}, bf16[16,256,16]{1,2,0:T(8,128)(2,1)S(1)}, u32[]{:S(2)}, u32[]{:S(2)}) collective-permute-start(bf16[16,256,16]{1,2,0:T(8,128)(2,1)} %bitcast.104), channel_id=1, source_target_pairs={{0,3},{1,2},{2,1},{3,0},{4,7},{5,6},{6,5},{7,4},{8,11},{9,10},{10,... | collective-permute-start | bytes 393224 | tf_op jit(solution)/shard_map/ppermute | solution.py:81
  345.0 48.8 %collective-permute-start.10 = (bf16[16,256,16]{1,2,0:T(8,128)(2,1)}, bf16[16,256,16]{1,2,0:T(8,128)(2,1)}, u32[]{:S(2)}, u32[]{:S(2)}) collective-permute-start(bf16[16,256,16]{1,2,0:T(8,128)(2,1)} %bitcast.103), channel_id=1, source_target_pairs={{0,4},{1,5},{2,6},{3,7},{4,0},{5,1},{6,2},{7,3},{8,12},{9,13},{10,... | collective-permute-start | bytes 393224 | tf_op jit(solution)/shard_map/ppermute | solution.py:81
  348.7 47.4 %collective-permute-start.11 = (bf16[16,256,16]{1,2,0:T(8,128)(2,1)}, bf16[16,256,16]{1,2,0:T(8,128)(2,1)}, u32[]{:S(2)}, u32[]{:S(2)}) collective-permute-start(bf16[16,256,16]{1,2,0:T(8,128)(2,1)} %bitcast.102), channel_id=1, source_target_pairs={{0,5},{1,4},{2,7},{3,6},{4,1},{5,0},{6,3},{7,2},{8,13},{9,12},{10,... | collective-permute-start | bytes 393224 | tf_op jit(solution)/shard_map/ppermute | solution.py:81
  349.1 49.2 %collective-permute-start.12 = (bf16[16,256,16]{1,2,0:T(8,128)(2,1)}, bf16[16,256,16]{1,2,0:T(8,128)(2,1)}, u32[]{:S(2)}, u32[]{:S(2)}) collective-permute-start(bf16[16,256,16]{1,2,0:T(8,128)(2,1)} %bitcast.101), channel_id=1, source_target_pairs={{0,6},{1,7},{2,4},{3,5},{4,2},{5,3},{6,0},{7,1},{8,14},{9,15},{10,... | collective-permute-start | bytes 393224 | tf_op jit(solution)/shard_map/ppermute | solution.py:81
  353.4 47.1 %collective-permute-start.13 = (bf16[16,256,16]{1,2,0:T(8,128)(2,1)}, bf16[16,256,16]{1,2,0:T(8,128)(2,1)}, u32[]{:S(2)}, u32[]{:S(2)}) collective-permute-start(bf16[16,256,16]{1,2,0:T(8,128)(2,1)} %bitcast.100), channel_id=1, source_target_pairs={{0,7},{1,6},{2,5},{3,4},{4,3},{5,2},{6,1},{7,0},{8,15},{9,14},{10,... | collective-permute-start | bytes 393224 | tf_op jit(solution)/shard_map/ppermute | solution.py:81
  534.1 23.5 %copy-start.7 = (bf16[1,16,256,16]{3,2,1,0:T(8,128)(2,1)S(1)}, bf16[1,16,256,16]{3,2,1,0:T(8,128)(2,1)}, u32[]{:S(2)}) copy-start(bf16[1,16,256,16]{3,2,1,0:T(8,128)(2,1)} %copy.59) | copy-start | bytes 393220
  (10 other events, 89.6 us)
Sparse Core Ops, SparseCore 0:
  10.6 37.1 all-gather.7
  49.9 124.9 all-gather.9
  176.4 41.4 all-gather.5
